TPU v7x, 32 devices: a whole 2x2x4 slice. The times are simulated.
32 devices in a mesh: wide: 16 (over z, y, core), narrow: 2 (over x).
Axes of the slice: x: 2, y: 2, z: 4, core: 2. Of those that a mesh axis runs over, the one named last changes fastest.
Arguments:
- valence: float32 [8, 32768], P(None, ('wide', 'narrow')), may hold values from -6 to 6
- conduction: float32 [32, 32768], P(('wide', 'narrow')), may hold values from -6 to 6
- eps_val: float32 [8], replicated, may hold values from -12 to -2
- eps_cond: float32 [32], replicated, may hold values from 0.5 to 20
- omega: float32 [6], replicated, may hold values from 0.3 to 30
- gmap: int32 [8192], replicated, may hold values from 0 to 32767, as said below
Outputs:
- chi: float32 [6, 8192, 8192], P(None, 'wide', 'narrow')
Inputs may be any that keep to these rules, and one draw needn't show every extreme that they name: `gmap`: distinct grid indices: the 8192 grid points of smallest squared wave vector (frequencies folded to -16 .. 15), equal lengths in random order, listed by rising length.
All inputs are finite; a program needn't handle non-finite values.
Results may differ from a plain program's by a relative error of at most 0.0042.
Values may be sent and summed in bfloat16 or wider, within the bound.
A program may use at most 128 MiB of HBM per device.

v0:
```python
import functools
import math

import jax
import jax.numpy as jnp
import numpy as np
from jax import lax
from jax.experimental import pallas as pl
from jax.experimental.pallas import tpu as pltpu
from jax.sharding import PartitionSpec as P

GRID = 32
MESH = pl.DeviceIdType.MESH
VMEM = pltpu.MemorySpace.VMEM


def wide_factors(wide):
    chips = wide // 2
    inner = 2 ** (int(math.log2(chips)) // 2)
    return chips // inner, inner


def gather_kernel(wide, narrow, split, row_width, src, out, *rest):
    if row_width:
        rows, send_sem, recv_sem, own_sem, row_send, row_recv = rest
    else:
        send_sem, recv_sem, own_sem = rest
    outer, inner = wide_factors(wide)
    w, n = lax.axis_index("wide"), lax.axis_index("narrow")
    core = lax.rem(w, 2)
    y = lax.rem(w // 2, inner)
    z = w // (2 * inner)

    def wide_at(zz, yy, cc):
        return (zz * inner + yy) * 2 + cc

    def slot(zz, yy, cc, nn):
        return wide_at(zz, yy, cc) * narrow + nn

    xs = [lax.rem(n + i, narrow) for i in range(1, narrow)]
    zs = [lax.rem(z + i, outer) for i in range(1, outer)]
    ys = [lax.rem(y + i, inner) for i in range(1, inner)]
    to_x = [(w, nn) for nn in xs]
    to_z = [(wide_at(zz, y, core), n) for zz in zs]
    to_y = [(wide_at(z, yy, core), n) for yy in ys]
    to_core = [(wide_at(z, y, 1 - core), n)]
    peers = to_x + to_z + to_y + to_core

    barrier = pltpu.get_barrier_semaphore()
    for peer in peers:
        pl.semaphore_signal(barrier, inc=1, device_id=peer, device_id_type=MESH)
    pl.semaphore_wait(barrier, len(peers))

    def piece(nn):
        if split:
            return src.at[:, pl.ds(pl.multiple_of(nn * split, split), split)]
        return src

    started = []

    def send(ref, index, target):
        copy = pltpu.make_async_remote_copy(
            src_ref=ref,
            dst_ref=out.at[index],
            send_sem=send_sem.at[len(started)],
            recv_sem=recv_sem.at[index],
            device_id=target,
            device_id_type=MESH,
        )
        copy.start()
        started.append(copy)

    def arrived(index):
        pltpu.make_async_remote_copy(
            src_ref=out.at[index],
            dst_ref=out.at[index],
            send_sem=send_sem.at[0],
            recv_sem=recv_sem.at[index],
            device_id=to_core[0],
            device_id_type=MESH,
        ).wait_recv()

    mine = slot(z, y, core, n)
    for target in to_x:
        send(piece(target[1]), mine, target)
    for target in to_z + to_y + to_core:
        send(piece(n), mine, target)
    own = pltpu.make_async_copy(piece(n), out.at[mine], own_sem)
    own.start()
    for nn in xs:
        index = slot(z, y, core, nn)
        arrived(index)
        for target in to_z + to_y + to_core:
            send(out.at[index], index, target)
    for zz in zs:
        for nn in [n] + xs:
            index = slot(zz, y, core, nn)
            arrived(index)
            for target in to_y + to_core:
                send(out.at[index], index, target)
    for yy in ys:
        for zz in [z] + zs:
            for nn in [n] + xs:
                index = slot(zz, yy, core, nn)
                arrived(index)
                send(out.at[index], index, to_core[0])
    own.wait()

    if row_width:
        holder = w // (wide // narrow)
        first = pl.multiple_of(lax.rem(w, wide // narrow) * row_width, 128)
        group = 2 * narrow

    def row_copy(index, target, start, sem):
        return pltpu.make_async_remote_copy(
            src_ref=out.at[pl.ds(start, group), :, pl.ds(first, row_width)],
            dst_ref=rows.at[pl.ds(start, group)],
            send_sem=row_send.at[sem],
            recv_sem=row_recv.at[index],
            device_id=target,
            device_id_type=MESH,
        )

    chips = [(zz, yy) for yy in [y] + ys for zz in [z] + zs]
    for number, (zz, yy) in enumerate(chips):
        for nn in [n] + xs:
            arrived(slot(zz, yy, 1 - core, nn))
        if row_width:
            @pl.when(n == holder)
            def _():
                for k, target in enumerate(to_x):
                    row_copy(number, target, slot(zz, yy, 0, 0), number * len(to_x) + k).start()

    for copy in started:
        copy.wait_send()
    if row_width:
        @pl.when(n == holder)
        def _():
            rows[...] = out[:, :, pl.ds(first, row_width)]
            for number, (zz, yy) in enumerate(chips):
                for k, target in enumerate(to_x):
                    row_copy(number, target, slot(zz, yy, 0, 0), number * len(to_x) + k).wait_send()

        @pl.when(n != holder)
        def _():
            for number, (zz, yy) in enumerate(chips):
                row_copy(number, to_x[0], slot(zz, yy, 0, 0), 0).wait_recv()


def gather(src, wide, narrow, split, row_width, collective_id):
    outer, inner = wide_factors(wide)
    devices = wide * narrow
    n_x, n_z, n_y = narrow - 1, outer - 1, inner - 1
    sends = n_x + n_z + n_y + 1
    sends += n_x * (n_z + n_y + 1) + n_z * narrow * (n_y + 1) + n_y * outer * narrow
    block = (src.shape[0], split or src.shape[1])
    out_shape = [jax.ShapeDtypeStruct((devices,) + block, src.dtype)]
    scratch = [
        pltpu.SemaphoreType.DMA((sends,)),
        pltpu.SemaphoreType.DMA((devices,)),
        pltpu.SemaphoreType.DMA,
    ]
    if row_width:
        out_shape.append(jax.ShapeDtypeStruct((devices, src.shape[0], row_width), src.dtype))
        scratch.append(pltpu.SemaphoreType.DMA((outer * inner * n_x,)))
        scratch.append(pltpu.SemaphoreType.DMA((outer * inner,)))
    return pl.pallas_call(
        functools.partial(gather_kernel, wide, narrow, split, row_width),
        out_shape=out_shape,
        in_specs=[pl.BlockSpec(memory_space=VMEM)],
        out_specs=[pl.BlockSpec(memory_space=VMEM)] * len(out_shape),
        scratch_shapes=scratch,
        compiler_params=pltpu.CompilerParams(
            collective_id=collective_id, has_side_effects=True, vmem_limit_bytes=48 << 20
        ),
    )(src)


@functools.lru_cache(None)
def tables(num_waves, num_val):
    fold = np.arange(GRID)
    fold = np.where(fold < GRID // 2, fold, fold - GRID)
    squares = fold**2
    lengths = (squares[:, None, None] + squares[None, :, None] + squares[None, None, :]).reshape(-1)
    limit = int(np.sort(lengths)[num_waves - 1])
    reach = math.isqrt(limit)
    assert reach < GRID // 2
    half = [
        (ky, kz)
        for ky in range(-reach, reach + 1)
        for kz in range(0, reach + 1)
        if ky * ky + kz * kz <= limit and (kz > 0 or ky >= 0)
    ]
    count = -(-len(half) // 128) * 128
    kys = np.array([k for k, _ in half])
    kzs = np.array([k for _, k in half])
    points = np.arange(GRID)
    turn = 2.0 * np.pi / GRID
    phase = (points[:, None, None] * kys + points[None, :, None] * kzs) % GRID
    phase = phase.reshape(GRID * GRID, len(half)) * turn
    plane = np.zeros((GRID * GRID, 2 * count))
    plane[:, : len(half)] = np.cos(phase)
    plane[:, count : count + len(half)] = -np.sin(phase)
    codes = np.full((count, 2), -1, np.int32)
    codes[: len(half), 0] = (kys % GRID) * GRID + kzs % GRID
    codes[: len(half), 1] = (-kys % GRID) * GRID + -kzs % GRID
    kxs = np.arange(-reach, reach + 1)
    line = (kxs[:, None] * points[None, :] % GRID) * turn
    eye = np.eye(num_val)
    norm = 1.0 / math.sqrt(GRID**3)
    cosine = np.kron(np.cos(line), eye) * norm
    sine = np.kron(np.sin(line), eye) * norm
    return plane, codes, np.stack([cosine, sine]), reach


def np_halves(table):
    table = np.asarray(table, np.float32)
    high = table.astype(jnp.bfloat16)
    return high, (table - high.astype(np.float32)).astype(jnp.bfloat16)


def split_bf16(x):
    high = x.astype(jnp.bfloat16)
    return high, (x - high.astype(jnp.float32)).astype(jnp.bfloat16)


def dot(a, b):
    return jnp.dot(a, b, preferred_element_type=jnp.float32)


def dot3(a, b_high, b_low):
    a_high, a_low = split_bf16(a)
    return dot(a_high, b_high) + (dot(a_low, b_high) + dot(a_high, b_low))


def dot3_left(a_high, a_low, b):
    b_high, b_low = split_bf16(b)
    return dot(a_high, b_high) + (dot(a_high, b_low) + dot(a_low, b_high))


def pair_kernel(reach, tile, val, cond, gmap, plane_h, plane_l, codes, line_h, line_l, out, field, picked):
    xs, num_val, plane = val.shape
    count = codes.shape[0]
    kinds = 2 * reach + 1
    field[...] = (val[...] * cond[...]).reshape(xs * num_val, plane)
    step = dot3(field[...], plane_h[...], plane_l[...])
    real, imag = step[:, :count], step[:, count:]
    size = kinds * num_val
    cos_h, sin_h, cos_l, sin_l = line_h[0], line_h[1], line_l[0], line_l[1]
    picked[:size, :] = dot3_left(cos_h, cos_l, real) + dot3_left(sin_h, sin_l, imag)
    picked[size:, :] = dot3_left(cos_h, cos_l, imag) - dot3_left(sin_h, sin_l, real)
    source = picked[...].astype(jnp.bfloat16)
    first, second = codes[:, 0:1], codes[:, 1:2]

    def body(t, carry):
        here = pl.ds(pl.multiple_of(t * tile, tile), tile)
        index = gmap[:, here]
        kx = index // (GRID * GRID)
        code = index % (GRID * GRID)
        ky, kz = code // GRID, code % GRID
        kx = jnp.where(kx < GRID // 2, kx, kx - GRID)
        direct = ((kz > 0) & (kz < GRID // 2)) | ((kz == 0) & (ky < GRID // 2))
        kx = jnp.where(direct, kx, -kx) + reach
        sign = jnp.where(direct, 1.0, -1.0).astype(jnp.float32)
        hit = (code == first) | (code == second)
        columns = dot(source, jnp.where(hit, 1.0, 0.0).astype(jnp.bfloat16))
        columns = columns.reshape(2, kinds, num_val, tile)
        real = jnp.zeros((num_val, tile), jnp.float32)
        imag = jnp.zeros((num_val, tile), jnp.float32)
        for k in range(kinds):
            keep = jnp.broadcast_to(kx == k, (num_val, tile))
            real = jnp.where(keep, columns[0, k], real)
            imag = jnp.where(keep, columns[1, k], imag)
        out[:, here] = jnp.concatenate([real, imag * sign], axis=0).astype(jnp.bfloat16)
        return carry

    lax.fori_loop(0, out.shape[1] // tile, body, 0)


def transform_pairs(val, cond, gmap):
    xs, num_val, plane = val.shape
    waves = gmap.shape[1]
    table, codes, line, reach = tables(waves, num_val)
    plane_h, plane_l = np_halves(table)
    line_h, line_l = np_halves(line)
    count = codes.shape[0]
    return pl.pallas_call(
        functools.partial(pair_kernel, reach, min(512, waves)),
        out_shape=jax.ShapeDtypeStruct((2 * num_val, waves), jnp.bfloat16),
        in_specs=[pl.BlockSpec(memory_space=VMEM)] * 8,
        out_specs=pl.BlockSpec(memory_space=VMEM),
        scratch_shapes=[
            pltpu.VMEM((xs * num_val, plane), jnp.float32),
            pltpu.VMEM((2 * (2 * reach + 1) * num_val, count), jnp.float32),
        ],
        compiler_params=pltpu.CompilerParams(vmem_limit_bytes=48 << 20),
    )(val, cond, gmap, jnp.asarray(plane_h), jnp.asarray(plane_l), jnp.asarray(codes), jnp.asarray(line_h), jnp.asarray(line_l))


def chi_kernel(weights, rows, columns, out, scaled):
    @pl.when(pl.program_id(1) == 0)
    def _():
        scale = rows[...].astype(jnp.float32) * weights[0]
        scaled[...] = scale.T.astype(jnp.bfloat16)

    out[0] = dot(scaled[...], columns[...])


def chi_of(weights, rows, columns):
    depth, row_width = rows.shape
    width = columns.shape[1]
    num = weights.shape[0]
    tile = min(1024, width)
    return pl.pallas_call(
        chi_kernel,
        grid=(num, width // tile),
        out_shape=jax.ShapeDtypeStruct((num, row_width, width), jnp.float32),
        in_specs=[
            pl.BlockSpec((1, depth, 1), lambda w, c: (w, 0, 0)),
            pl.BlockSpec((depth, row_width), lambda w, c: (0, 0)),
            pl.BlockSpec((depth, tile), lambda w, c: (0, c)),
        ],
        out_specs=pl.BlockSpec((1, row_width, tile), lambda w, c: (w, 0, c)),
        scratch_shapes=[pltpu.VMEM((row_width, depth), jnp.bfloat16)],
        compiler_params=pltpu.CompilerParams(vmem_limit_bytes=48 << 20),
    )(weights, rows, columns)


def body(valence, conduction, eps_val, eps_cond, omega, gmap):
    wide, narrow = lax.axis_size("wide"), lax.axis_size("narrow")
    devices = wide * narrow
    num_val, chunk = valence.shape
    num_local = conduction.shape[0]
    assert num_local == 1
    plane = GRID * GRID
    waves = gmap.shape[0]
    [full] = gather(valence, wide, narrow, 0, 0, 0)
    if chunk != plane:
        full = full.reshape(GRID, devices // GRID, num_val, chunk)
        full = jnp.transpose(full, (0, 2, 1, 3)).reshape(GRID, num_val, plane)
    local = transform_pairs(full, conduction.reshape(GRID, 1, plane), gmap.reshape(1, waves))
    columns, rows = gather(local, wide, narrow, waves // narrow, waves // wide, 1)
    depth = devices * 2 * num_val
    columns = columns.reshape(depth, waves // narrow)
    rows = rows.reshape(depth, waves // wide)
    num_pairs = num_val * eps_cond.shape[0]
    gap = eps_cond[:, None] - eps_val[None, :]
    gap = jnp.stack([gap, gap], axis=1).reshape(depth)
    weights = -2.0 * gap[None, :] / (gap[None, :] ** 2 + omega[:, None] ** 2)
    weights = weights / jnp.sqrt(jnp.float32(num_pairs))
    return chi_of(weights[:, :, None], rows, columns)


def solution(mesh):
    placed = (P(None, ("wide", "narrow")), P(("wide", "narrow"), None), P(), P(), P(), P())
    return jax.shard_map(
        body, mesh=mesh, in_specs=placed, out_specs=P(None, "wide", "narrow"), check_vma=False
    )
```

profile of v0, /device:TPU:14, one launch (start us, length us, event | category | flops | bytes accessed | tf_op | source)
XLA Modules:
  0.0 126.3 jit_solution(4910736944987396136)
XLA Ops:
  0.0 0.0 copy-start.1
  0.0 0.8 integer_pow.17
  0.8 0.7 broadcast_subtract_fusion
  1.5 0.1 copy.15
  1.6 0.1 integer_pow.16
  1.7 0.1 copy.14
  1.8 0.1 mul.16
  1.9 0.0 copy-start.8
  1.9 0.8 copy-done.8
  2.7 14.8 %shard_map.109.val = f32[32,8,1024]{2,1,0:T(8,128)S(1)} custom-call(f32[8,1024]{1,0:T(8,128)S(1)} %copy-done.8), custom_call_target="tpu_custom_call" | custom-call | tf_op jit(solution)/shard_map/pallas_call | solution.py:167
  17.5 0.0 copy-done.1
  17.5 0.0 copy-start.2
  17.5 1.2 copy-done.2
  18.7 0.9 copy-done.3
  19.7 0.9 copy-done.4
  20.6 0.9 copy-done.5
  21.5 0.9 copy-done.6
  22.4 0.8 copy-done.7
  23.2 8.3 %shard_map.110.src = bf16[16,8192]{1,0:T(8,128)(2,1)S(1)} custom-call(f32[32,8,1024]{2,1,0:T(8,128)S(1)} %shard_map.109.val, f32[32,1,1024]{2,1,0:T(1,128)S(1)} %bitcast.6, s32[1,8192]{1,0:T(1,128)S(1)} %bitcast.7, bf16[1024,512]{1,0:T(8,128)(2,1)S(1)} %copy-done.2, bf16[1024,512]{1,0:T(8,128)(2,1)S(1)} %copy-done.1, s32[256,2]{1,0:T(8,128)S(1)} %copy-done.6, ...), custom_call_target="tpu_custom_call" | custom-call | tf_op jit(solution)/shard_map/pallas_call | solution.py:287
  31.5 0.3 divide_multiply_fusion.weights
  31.8 56.1 %shard_map.111 = (bf16[32,16,4096]{2,1,0:T(8,128)(2,1)S(1)}, bf16[32,16,512]{2,1,0:T(8,128)(2,1)S(1)}) custom-call(bf16[16,8192]{1,0:T(8,128)(2,1)S(1)} %shard_map.110.src), custom_call_target="tpu_custom_call" | custom-call | tf_op jit(solution)/shard_map/pallas_call | solution.py:167
  87.9 0.0 copy-start
  87.9 1.9 %copy-done = bf16[32,16,4096]{2,1,0:T(8,128)(2,1)} copy-done((bf16[32,16,4096]{2,1,0:T(8,128)(2,1)}, bf16[32,16,4096]{2,1,0:T(8,128)(2,1)S(1)}, u32[]{:S(2)}) %copy-start) | copy-done | bytes 4194328
  89.8 36.5 %shard_map.112 = f32[6,512,4096]{2,1,0:T(8,128)} custom-call(f32[6,512,1]{2,1,0:T(8,128)S(1)} %divide_multiply_fusion.weights, bf16[512,512]{1,0:T(8,128)(2,1)S(1)} %bitcast.5, bf16[512,4096]{1,0:T(8,128)(2,1)} %bitcast.4), custom_call_target="tpu_custom_call" | custom-call | tf_op jit(solution)/shard_map/pallas_call | solution.py:314
  (6 shorter events, 0.0 us)
Async XLA Ops:
  0.0 17.5 %copy-start.1 = (bf16[1024,512]{1,0:T(8,128)(2,1)S(1)}, bf16[1024,512]{1,0:T(8,128)(2,1)}, u32[]{:S(2)}) copy-start(bf16[1024,512]{1,0:T(8,128)(2,1)} %constant.16.clone.plane_l) | copy-start | bytes 3145732
  1.9 0.8 copy-start.8
  17.5 1.2 copy-start.2
  18.7 0.9 copy-start.3
  19.7 0.9 copy-start.4
  20.6 0.9 copy-start.5
  21.5 0.9 copy-start.6
  22.4 0.8 copy-start.7
  87.9 1.9 %copy-start = (bf16[32,16,4096]{2,1,0:T(8,128)(2,1)}, bf16[32,16,4096]{2,1,0:T(8,128)(2,1)S(1)}, u32[]{:S(2)}) copy-start(bf16[32,16,4096]{2,1,0:T(8,128)(2,1)S(1)} %get-tuple-element.8) | copy-start | bytes 12582916
where the time goes:
time: 128 us; the launch traced here: 126 us
  Pallas kernels  116 us (91%)
  local copies, waits for them, and re-layouts  8.74 us (7%)
  other arithmetic  1.8 us (1%)
    pallas_call x2, Pallas kernels, gather(): pl.pallas_call(functools.partial(gather_kernel, wide, narrow, split, row_...  70.9 us
    pallas_call x1, Pallas kernels, chi_of(): pl.pallas_call(chi_kernel, grid=(num, width // tile), out_shape=jax.Shape...  36.5 us
    unnamed x18, local copies, waits for them, and re-layouts  8.35 us
    pallas_call x1, Pallas kernels, transform_pairs(): pl.pallas_call(functools.partial(pair_kernel, reach, min(512, waves)), ou...  8.33 us

commit v1 on v0

--- a/solution.py
+++ b/solution.py
@@ -12,6 +12,8 @@
 GRID = 32
 MESH = pl.DeviceIdType.MESH
 VMEM = pltpu.MemorySpace.VMEM
+HBM = pltpu.MemorySpace.HBM
+SMEM = pltpu.MemorySpace.SMEM
 
 
 def wide_factors(wide):
@@ -167,11 +169,11 @@
     return pl.pallas_call(
         functools.partial(gather_kernel, wide, narrow, split, row_width),
         out_shape=out_shape,
-        in_specs=[pl.BlockSpec(memory_space=VMEM)],
-        out_specs=[pl.BlockSpec(memory_space=VMEM)] * len(out_shape),
+        in_specs=[pl.BlockSpec(memory_space=pl.ANY)],
+        out_specs=[pl.BlockSpec(memory_space=VMEM if row_width else pl.ANY)] * len(out_shape),
         scratch_shapes=scratch,
         compiler_params=pltpu.CompilerParams(
-            collective_id=collective_id, has_side_effects=True, vmem_limit_bytes=48 << 20
+            collective_id=collective_id, has_side_effects=True, vmem_limit_bytes=(48 if row_width else 63) << 20
         ),
     )(src)
 
@@ -238,7 +240,15 @@
     return dot(a_high, b_high) + (dot(a_high, b_low) + dot(a_low, b_high))
 
 
-def pair_kernel(reach, tile, val, cond, gmap, plane_h, plane_l, codes, line_h, line_l, out, field, picked):
+def pair_kernel(reach, tile, *refs):
+    sources, out, field, picked = refs[:8], refs[8], refs[9], refs[10]
+    held, sems = refs[11:19], refs[19]
+    copies = [pltpu.make_async_copy(a, b, sems.at[i]) for i, (a, b) in enumerate(zip(sources, held))]
+    for copy in copies:
+        copy.start()
+    val, cond, plane_h, plane_l, line_h, line_l, codes, gmap = held
+    for copy in copies:
+        copy.wait()
     xs, num_val, plane = val.shape
     count = codes.shape[0]
     kinds = 2 * reach + 1
@@ -284,46 +294,71 @@
     plane_h, plane_l = np_halves(table)
     line_h, line_l = np_halves(line)
     count = codes.shape[0]
+    operands = (val, cond, plane_h, plane_l, line_h, line_l, codes, gmap)
+    held = [pltpu.VMEM(x.shape, x.dtype) for x in operands]
     return pl.pallas_call(
         functools.partial(pair_kernel, reach, min(512, waves)),
         out_shape=jax.ShapeDtypeStruct((2 * num_val, waves), jnp.bfloat16),
-        in_specs=[pl.BlockSpec(memory_space=VMEM)] * 8,
+        in_specs=[pl.BlockSpec(memory_space=pl.ANY)] * 8,
         out_specs=pl.BlockSpec(memory_space=VMEM),
         scratch_shapes=[
             pltpu.VMEM((xs * num_val, plane), jnp.float32),
             pltpu.VMEM((2 * (2 * reach + 1) * num_val, count), jnp.float32),
-        ],
-        compiler_params=pltpu.CompilerParams(vmem_limit_bytes=48 << 20),
-    )(val, cond, gmap, jnp.asarray(plane_h), jnp.asarray(plane_l), jnp.asarray(codes), jnp.asarray(line_h), jnp.asarray(line_l))
-
-
-def chi_kernel(weights, rows, columns, out, scaled):
-    @pl.when(pl.program_id(1) == 0)
+        ]
+        + held
+        + [pltpu.SemaphoreType.DMA((8,))],
+        compiler_params=pltpu.CompilerParams(vmem_limit_bytes=62 << 20),
+    )(*[jnp.asarray(x) for x in operands])
+
+
+def chi_kernel(num_cond, num_val, scalars, rows, columns, out, scaled):
+    num = out.shape[0]
+
+    @pl.when(pl.program_id(0) == 0)
     def _():
-        scale = rows[...].astype(jnp.float32) * weights[0]
-        scaled[...] = scale.T.astype(jnp.bfloat16)
-
-    out[0] = dot(scaled[...], columns[...])
-
-
-def chi_of(weights, rows, columns):
+        depth = rows.shape[0]
+        lane = lax.broadcasted_iota(jnp.int32, (1, depth), 1)
+        band, orbital = lane // (2 * num_val), lane % num_val
+
+        def pick(first, count, where):
+            def step(i, held):
+                return jnp.where(where == i, scalars[first + i], held)
+
+            return lax.fori_loop(0, count, step, jnp.zeros((1, depth), jnp.float32))
+
+        gap = pick(0, num_cond, band) - pick(num_cond, num_val, orbital)
+        norm = math.sqrt(num_cond * num_val)
+        turned = rows[...].astype(jnp.float32).T
+        for w in range(num):
+            omega = scalars[num_cond + num_val + w]
+            weight = -2.0 * gap / (gap * gap + omega * omega) / norm
+            scaled[w] = (turned * weight).astype(jnp.bfloat16)
+
+    for w in range(num):
+        out[w] = dot(scaled[w], columns[...])
+
+
+def chi_of(eps_cond, eps_val, omega, rows, columns):
     depth, row_width = rows.shape
     width = columns.shape[1]
-    num = weights.shape[0]
-    tile = min(1024, width)
+    num = omega.shape[0]
+    tile = min(512, width)
+    grant = 4 * depth * (row_width + tile) + 8 * num * row_width * tile
+    grant += (2 * num + 12) * row_width * depth + (8 << 20)
+    scalars = jnp.concatenate([eps_cond, eps_val, omega])
     return pl.pallas_call(
-        chi_kernel,
-        grid=(num, width // tile),
+        functools.partial(chi_kernel, eps_cond.shape[0], eps_val.shape[0]),
+        grid=(width // tile,),
         out_shape=jax.ShapeDtypeStruct((num, row_width, width), jnp.float32),
-        in_specs=[
-            pl.BlockSpec((1, depth, 1), lambda w, c: (w, 0, 0)),
-            pl.BlockSpec((depth, row_width), lambda w, c: (0, 0)),
-            pl.BlockSpec((depth, tile), lambda w, c: (0, c)),
+        in_specs=[pl.BlockSpec(memory_space=SMEM)]
+        + [
+            pl.BlockSpec((depth, row_width), lambda c: (0, 0)),
+            pl.BlockSpec((depth, tile), lambda c: (0, c)),
         ],
-        out_specs=pl.BlockSpec((1, row_width, tile), lambda w, c: (w, 0, c)),
-        scratch_shapes=[pltpu.VMEM((row_width, depth), jnp.bfloat16)],
-        compiler_params=pltpu.CompilerParams(vmem_limit_bytes=48 << 20),
-    )(weights, rows, columns)
+        out_specs=pl.BlockSpec((num, row_width, tile), lambda c: (0, 0, c)),
+        scratch_shapes=[pltpu.VMEM((num, row_width, depth), jnp.bfloat16)],
+        compiler_params=pltpu.CompilerParams(vmem_limit_bytes=grant),
+    )(scalars, rows, columns)
 
 
 def body(valence, conduction, eps_val, eps_cond, omega, gmap):
@@ -343,12 +378,7 @@
     depth = devices * 2 * num_val
     columns = columns.reshape(depth, waves // narrow)
     rows = rows.reshape(depth, waves // wide)
-    num_pairs = num_val * eps_cond.shape[0]
-    gap = eps_cond[:, None] - eps_val[None, :]
-    gap = jnp.stack([gap, gap], axis=1).reshape(depth)
-    weights = -2.0 * gap[None, :] / (gap[None, :] ** 2 + omega[:, None] ** 2)
-    weights = weights / jnp.sqrt(jnp.float32(num_pairs))
-    return chi_of(weights[:, :, None], rows, columns)
+    return chi_of(eps_cond, eps_val, omega, rows, columns)
 
 
 def solution(mesh):

time: 128 us -> 107 us (0.84); the launches traced: 126 us -> 107 us
  Pallas kernels: 116 us -> 105 us
  local copies, waits for them, and re-layouts: 8.74 us -> 0.95 us
    pallas_call x1, Pallas kernels: 36.5 us -> 21.8 us  [chi_of(): pl.pallas_call(functools.partial(chi_kernel, eps_cond.shape[0], eps_val.s...]
    unnamed x18 -> x2, local copies, waits for them, and re-layouts: 8.35 us -> 0.95 us
    pallas_call x1, Pallas kernels: 8.33 us -> 11.1 us  [transform_pairs(): pl.pallas_call(functools.partial(pair_kernel, reach, min(512, waves)), ou...]
where the time goes in v1:
time: 107 us
  Pallas kernels  105 us (98%)
    pallas_call x2, Pallas kernels, gather(): pl.pallas_call(functools.partial(gather_kernel, wide, narrow, split, row_...  72 us
    pallas_call x1, Pallas kernels, chi_of(): pl.pallas_call(functools.partial(chi_kernel, eps_cond.shape[0], eps_val.s...  21.8 us
    pallas_call x1, Pallas kernels, transform_pairs(): pl.pallas_call(functools.partial(pair_kernel, reach, min(512, waves)), ou...  11.1 us

profile of v1, /device:TPU:14, one launch (start us, length us, event | category | flops | bytes accessed | tf_op | source)
XLA Modules:
  0.0 106.7 jit_solution(702030070951454401)
XLA Ops:
  0.0 0.8 pad_maximum_fusion.scalars
  0.8 15.7 %shard_map.109.refs_0_ = f32[32,8,1024]{2,1,0:T(8,128)} custom-call(f32[8,1024]{1,0:T(8,128)} %src.1), custom_call_target="tpu_custom_call" | custom-call | tf_op jit(solution)/shard_map/pallas_call | solution.py:169
  16.5 11.1 %shard_map.110.src = bf16[16,8192]{1,0:T(8,128)(2,1)} custom-call(f32[32,8,1024]{2,1,0:T(8,128)} %shard_map.109.refs_0_, f32[32,1,1024]{2,1,0:T(1,128)} %bitcast.6, bf16[1024,512]{1,0:T(8,128)(2,1)} %constant.10.clone.refs_2_, bf16[1024,512]{1,0:T(8,128)(2,1)} %constant.11.clone.refs_3_, bf16[2,200,256]{2,1,0:T(8,128)(2,1)} %constant.12.clone.refs_4_, ...), custom_call_target="tpu_custom_call" | custom-call | tf_op jit(solution)/shard_map/pallas_call | solution.py:299
  27.6 0.0 copy-start
  27.6 0.9 copy-done
  28.6 56.3 %shard_map.111 = (bf16[32,16,4096]{2,1,0:T(8,128)(2,1)S(1)}, bf16[32,16,512]{2,1,0:T(8,128)(2,1)S(1)}) custom-call(bf16[16,8192]{1,0:T(8,128)(2,1)S(1)} %copy-done), custom_call_target="tpu_custom_call" | custom-call | tf_op jit(solution)/shard_map/pallas_call | solution.py:169
  84.9 21.8 %shard_map.112 = f32[6,512,4096]{2,1,0:T(8,128)} custom-call(f32[46]{0:T(128)S(1)} %pad_maximum_fusion.scalars, bf16[512,512]{1,0:T(8,128)(2,1)S(1)} %bitcast.5, bf16[512,4096]{1,0:T(8,128)(2,1)S(1)} %bitcast.4), custom_call_target="tpu_custom_call" | custom-call | tf_op jit(solution)/shard_map/pallas_call | solution.py:349
Async XLA Ops:
  27.6 1.0 copy-start

commit v2 on v1

--- a/solution.py
+++ b/solution.py
@@ -22,7 +22,7 @@
     return chips // inner, inner
 
 
-def gather_kernel(wide, narrow, split, row_width, src, out, *rest):
+def gather_kernel(wide, narrow, split, row_width, row_step, src, out, *rest):
     if row_width:
         rows, send_sem, recv_sem, own_sem, row_send, row_recv = rest
     else:
@@ -110,7 +110,7 @@
 
     if row_width:
         holder = w // (wide // narrow)
-        first = pl.multiple_of(lax.rem(w, wide // narrow) * row_width, 128)
+        first = pl.multiple_of(lax.rem(w, wide // narrow) * row_step, 128)
         group = 2 * narrow
 
     def row_copy(index, target, start, sem):
@@ -149,7 +149,7 @@
                 row_copy(number, to_x[0], slot(zz, yy, 0, 0), 0).wait_recv()
 
 
-def gather(src, wide, narrow, split, row_width, collective_id):
+def gather(src, wide, narrow, split, row_width, row_step, collective_id):
     outer, inner = wide_factors(wide)
     devices = wide * narrow
     n_x, n_z, n_y = narrow - 1, outer - 1, inner - 1
@@ -167,7 +167,7 @@
         scratch.append(pltpu.SemaphoreType.DMA((outer * inner * n_x,)))
         scratch.append(pltpu.SemaphoreType.DMA((outer * inner,)))
     return pl.pallas_call(
-        functools.partial(gather_kernel, wide, narrow, split, row_width),
+        functools.partial(gather_kernel, wide, narrow, split, row_width, row_step),
         out_shape=out_shape,
         in_specs=[pl.BlockSpec(memory_space=pl.ANY)],
         out_specs=[pl.BlockSpec(memory_space=VMEM if row_width else pl.ANY)] * len(out_shape),
@@ -215,6 +215,41 @@
     return plane, codes, np.stack([cosine, sine]), reach
 
 
+MARGIN = 128
+
+
+def window(tile):
+    return tile // 2 + 2 * MARGIN
+
+
+@functools.lru_cache(None)
+def half_lists(num_waves, narrow, tiles):
+    fold = np.arange(GRID)
+    fold = np.where(fold < GRID // 2, fold, fold - GRID)
+    kx, ky, kz = [k.reshape(-1) for k in np.meshgrid(fold, fold, fold, indexing="ij")]
+    lengths = kx * kx + ky * ky + kz * kz
+    ordered = np.sort(lengths)[:num_waves]
+    half = (kz > 0) | ((kz == 0) & ((ky > 0) | ((ky == 0) & (kx >= 0))))
+    chosen = np.nonzero(half & (lengths <= ordered[-1]))[0]
+    chosen = chosen[np.argsort(lengths[chosen], kind="stable")]
+    sizes = lengths[chosen]
+    part = num_waves // narrow
+    slots = part // 2 + 2 * MARGIN
+    lists = np.full((narrow, 1, slots), -1, np.int32)
+    for n in range(narrow):
+        begin = np.searchsorted(sizes, ordered[n * part])
+        end = np.searchsorted(sizes, ordered[(n + 1) * part - 1], side="right")
+        assert end - begin + MARGIN <= slots
+        lists[n, 0, MARGIN : MARGIN + end - begin] = chosen[begin:end]
+        for tile in tiles:
+            for t in range(part // tile):
+                g = n * part + t * tile
+                low = np.searchsorted(sizes, ordered[g]) - begin + MARGIN
+                high = np.searchsorted(sizes, ordered[g + tile - 1], side="right") - begin + MARGIN
+                assert t * tile // 2 <= low and high <= t * tile // 2 + window(tile)
+    return lists
+
+
 def np_halves(table):
     table = np.asarray(table, np.float32)
     high = table.astype(jnp.bfloat16)
@@ -287,17 +322,17 @@
     lax.fori_loop(0, out.shape[1] // tile, body, 0)
 
 
-def transform_pairs(val, cond, gmap):
+def transform_pairs(val, cond, gmap, num_waves):
     xs, num_val, plane = val.shape
     waves = gmap.shape[1]
-    table, codes, line, reach = tables(waves, num_val)
+    table, codes, line, reach = tables(num_waves, num_val)
     plane_h, plane_l = np_halves(table)
     line_h, line_l = np_halves(line)
     count = codes.shape[0]
     operands = (val, cond, plane_h, plane_l, line_h, line_l, codes, gmap)
     held = [pltpu.VMEM(x.shape, x.dtype) for x in operands]
     return pl.pallas_call(
-        functools.partial(pair_kernel, reach, min(512, waves)),
+        functools.partial(pair_kernel, reach, 256),
         out_shape=jax.ShapeDtypeStruct((2 * num_val, waves), jnp.bfloat16),
         in_specs=[pl.BlockSpec(memory_space=pl.ANY)] * 8,
         out_specs=pl.BlockSpec(memory_space=VMEM),
@@ -311,54 +346,90 @@
     )(*[jnp.asarray(x) for x in operands])
 
 
-def chi_kernel(num_cond, num_val, scalars, rows, columns, out, scaled):
-    num = out.shape[0]
-
-    @pl.when(pl.program_id(0) == 0)
+def expand(held, listed, index, num_val):
+    depth, slots = held.shape
+    tile = index.shape[1]
+    area = GRID * GRID
+    lx, ly, lz = listed // area, listed // GRID % GRID, listed % GRID
+    mirror = (GRID - lx) % GRID * area + (GRID - ly) % GRID * GRID + (GRID - lz) % GRID
+    mirror = jnp.where(listed < 0, -1, mirror)
+
+    def column(row):
+        turned = jnp.broadcast_to(row, (128, slots)).T
+        return jnp.concatenate([turned] * (tile // 128), axis=1)
+
+    hit = (index == column(listed)) | (index == column(mirror))
+    values = dot(held, jnp.where(hit, 1.0, 0.0).astype(jnp.bfloat16))
+    kx, ky, kz = index // area, index // GRID % GRID, index % GRID
+    low = GRID // 2
+    direct = ((kz > 0) & (kz < low)) | (
+        (kz == 0) & (((ky > 0) & (ky < low)) | ((ky == 0) & (kx < low)))
+    )
+    sign = jnp.where(direct, 1.0, -1.0).astype(jnp.float32)
+    row = lax.broadcasted_iota(jnp.int32, (depth, tile), 0)
+    return values * jnp.where(row // num_val % 2 == 1, sign, 1.0)
+
+
+def chi_kernel(num_cond, num_val, scalars, gmap, lists, rows, columns, out, scaled):
+    num, row_width, tile = out.shape
+    depth = rows.shape[0]
+    narrow, wide = lists.shape[0], gmap.shape[1] // row_width
+    w, n = lax.axis_index("wide"), lax.axis_index("narrow")
+    step = pl.program_id(0)
+
+    @pl.when(step == 0)
     def _():
-        depth = rows.shape[0]
         lane = lax.broadcasted_iota(jnp.int32, (1, depth), 1)
         band, orbital = lane // (2 * num_val), lane % num_val
 
         def pick(first, count, where):
-            def step(i, held):
+            def select(i, held):
                 return jnp.where(where == i, scalars[first + i], held)
 
-            return lax.fori_loop(0, count, step, jnp.zeros((1, depth), jnp.float32))
+            return lax.fori_loop(0, count, select, jnp.zeros((1, depth), jnp.float32))
 
         gap = pick(0, num_cond, band) - pick(num_cond, num_val, orbital)
         norm = math.sqrt(num_cond * num_val)
-        turned = rows[...].astype(jnp.float32).T
-        for w in range(num):
-            omega = scalars[num_cond + num_val + w]
+        first = pl.multiple_of(lax.rem(w, wide // narrow) * (row_width // 2), 128)
+        listed = lists[w // (wide // narrow), :, pl.ds(first, rows.shape[1])]
+        index = gmap[:, pl.ds(pl.multiple_of(w * row_width, 128), row_width)]
+        turned = expand(rows[...], listed, index, num_val).T
+        for i in range(num):
+            omega = scalars[num_cond + num_val + i]
             weight = -2.0 * gap / (gap * gap + omega * omega) / norm
-            scaled[w] = (turned * weight).astype(jnp.bfloat16)
-
-    for w in range(num):
-        out[w] = dot(scaled[w], columns[...])
-
-
-def chi_of(eps_cond, eps_val, omega, rows, columns):
-    depth, row_width = rows.shape
-    width = columns.shape[1]
+            scaled[i] = (turned * weight).astype(jnp.bfloat16)
+
+    first = pl.multiple_of(step * (tile // 2), 128)
+    here = pl.ds(first, window(tile))
+    part = gmap.shape[1] // narrow
+    index = gmap[:, pl.ds(pl.multiple_of(n * part + step * tile, 128), tile)]
+    panel = expand(columns[:, here], lists[n, :, here], index, num_val).astype(jnp.bfloat16)
+    for i in range(num):
+        out[i] = dot(scaled[i], panel)
+
+
+def chi_of(eps_cond, eps_val, omega, gmap, lists, rows, columns, row_width, width):
+    depth, row_slots = rows.shape
     num = omega.shape[0]
     tile = min(512, width)
-    grant = 4 * depth * (row_width + tile) + 8 * num * row_width * tile
-    grant += (2 * num + 12) * row_width * depth + (8 << 20)
+    grant = 4 * depth * (row_slots + columns.shape[1]) + 8 * num * row_width * tile
+    grant += (2 * num + 16) * row_width * depth + 16 * depth * tile + (8 << 20)
     scalars = jnp.concatenate([eps_cond, eps_val, omega])
     return pl.pallas_call(
         functools.partial(chi_kernel, eps_cond.shape[0], eps_val.shape[0]),
         grid=(width // tile,),
         out_shape=jax.ShapeDtypeStruct((num, row_width, width), jnp.float32),
-        in_specs=[pl.BlockSpec(memory_space=SMEM)]
-        + [
-            pl.BlockSpec((depth, row_width), lambda c: (0, 0)),
-            pl.BlockSpec((depth, tile), lambda c: (0, c)),
+        in_specs=[
+            pl.BlockSpec(memory_space=SMEM),
+            pl.BlockSpec(gmap.shape, lambda c: (0, 0)),
+            pl.BlockSpec(lists.shape, lambda c: (0, 0, 0)),
+            pl.BlockSpec(rows.shape, lambda c: (0, 0)),
+            pl.BlockSpec(columns.shape, lambda c: (0, 0)),
         ],
         out_specs=pl.BlockSpec((num, row_width, tile), lambda c: (0, 0, c)),
         scratch_shapes=[pltpu.VMEM((num, row_width, depth), jnp.bfloat16)],
-        compiler_params=pltpu.CompilerParams(vmem_limit_bytes=grant),
-    )(scalars, rows, columns)
+        compiler_params=pltpu.CompilerParams(vmem_limit_bytes=min(grant, 60 << 20)),
+    )(scalars, gmap, jnp.asarray(lists), rows, columns)
 
 
 def body(valence, conduction, eps_val, eps_cond, omega, gmap):
@@ -369,16 +440,20 @@
     assert num_local == 1
     plane = GRID * GRID
     waves = gmap.shape[0]
-    [full] = gather(valence, wide, narrow, 0, 0, 0)
+    [full] = gather(valence, wide, narrow, 0, 0, 0, 0)
     if chunk != plane:
         full = full.reshape(GRID, devices // GRID, num_val, chunk)
         full = jnp.transpose(full, (0, 2, 1, 3)).reshape(GRID, num_val, plane)
-    local = transform_pairs(full, conduction.reshape(GRID, 1, plane), gmap.reshape(1, waves))
-    columns, rows = gather(local, wide, narrow, waves // narrow, waves // wide, 1)
+    row_width, width = waves // wide, waves // narrow
+    lists = half_lists(waves, narrow, (row_width, min(512, width)))
+    wanted = np.maximum(lists.reshape(1, -1), 0)
+    local = transform_pairs(full, conduction.reshape(GRID, 1, plane), wanted, waves)
+    slots, row_slots = lists.shape[2], window(row_width)
+    columns, rows = gather(local, wide, narrow, slots, row_slots, row_width // 2, 1)
     depth = devices * 2 * num_val
-    columns = columns.reshape(depth, waves // narrow)
-    rows = rows.reshape(depth, waves // wide)
-    return chi_of(eps_cond, eps_val, omega, rows, columns)
+    columns, rows = columns.reshape(depth, slots), rows.reshape(depth, row_slots)
+    spot = gmap.reshape(1, waves)
+    return chi_of(eps_cond, eps_val, omega, spot, lists, rows, columns, row_width, width)
 
 
 def solution(mesh):

time: 107 us -> 94.4 us (0.88)
  Pallas kernels: 105 us -> 90.9 us
  local copies, waits for them, and re-layouts: 0.95 us -> 2.38 us
    pallas_call x2, Pallas kernels: 72 us -> 55.7 us  [gather(): pl.pallas_call(functools.partial(gather_kernel, wide, narrow, split, row_...]
    pallas_call x1, Pallas kernels: 21.8 us -> 24.4 us  [chi_of(): pl.pallas_call(functools.partial(chi_kernel, eps_cond.shape[0], eps_val.s...]
    unnamed x2 -> x6, local copies, waits for them, and re-layouts: 0.95 us -> 2.38 us
where the time goes in v2:
time: 94.4 us; the launch traced here: 94.1 us
  Pallas kernels  90.9 us (96%)
  local copies, waits for them, and re-layouts  2.38 us (3%)
    pallas_call x2, Pallas kernels, gather(): pl.pallas_call(functools.partial(gather_kernel, wide, narrow, split, row_...  55.7 us
    pallas_call x1, Pallas kernels, chi_of(): pl.pallas_call(functools.partial(chi_kernel, eps_cond.shape[0], eps_val.s...  24.4 us
    pallas_call x1, Pallas kernels, transform_pairs(): pl.pallas_call(functools.partial(pair_kernel, reach, 256), out_shape=jax....  10.8 us
    unnamed x6, local copies, waits for them, and re-layouts  2.38 us

profile of v2, /device:TPU:14, one launch (start us, length us, event | category | flops | bytes accessed | tf_op | source)
XLA Modules:
  0.0 94.1 jit_solution(11047378922265544229)
XLA Ops:
  0.0 0.8 pad_maximum_fusion.scalars
  0.8 15.7 %shard_map.127.refs_0_ = f32[32,8,1024]{2,1,0:T(8,128)} custom-call(f32[8,1024]{1,0:T(8,128)} %src.1), custom_call_target="tpu_custom_call" | custom-call | tf_op jit(solution)/shard_map/pallas_call | solution.py:169
  16.5 10.8 %shard_map.128.src = bf16[16,4608]{1,0:T(8,128)(2,1)} custom-call(f32[32,8,1024]{2,1,0:T(8,128)} %shard_map.127.refs_0_, f32[32,1,1024]{2,1,0:T(1,128)} %bitcast.7, bf16[1024,512]{1,0:T(8,128)(2,1)} %constant.14.clone.refs_2_, bf16[1024,512]{1,0:T(8,128)(2,1)} %constant.15.clone.refs_3_, bf16[2,200,256]{2,1,0:T(8,128)(2,1)} %constant.16.clone.refs_4_, ...), custom_call_target="tpu_custom_call" | custom-call | tf_op jit(solution)/shard_map/pallas_call | solution.py:334
  27.3 0.0 copy-start
  27.3 0.9 copy-done
  28.2 39.9 %shard_map.129 = (bf16[32,16,2304]{2,1,0:T(8,128)(2,1)S(1)}, bf16[32,16,512]{2,1,0:T(8,128)(2,1)S(1)}) custom-call(bf16[16,4608]{1,0:T(8,128)(2,1)S(1)} %copy-done), custom_call_target="tpu_custom_call" | custom-call | tf_op jit(solution)/shard_map/pallas_call | solution.py:169
  68.2 0.0 copy-start.1
  68.2 0.7 copy-done.1
  69.0 0.0 copy-start.2
  69.0 0.7 copy-done.2
  69.7 24.4 %shard_map.130 = f32[6,512,4096]{2,1,0:T(8,128)} custom-call(f32[46]{0:T(128)S(1)} %pad_maximum_fusion.scalars, s32[1,8192]{1,0:T(1,128)S(1)} %bitcast.6, s32[2,1,2304]{2,1,0:T(1,128)S(1)} %copy-done.2, bf16[512,512]{1,0:T(8,128)(2,1)S(1)} %bitcast.5, bf16[512,2304]{1,0:T(8,128)(2,1)S(1)} %bitcast.4), custom_call_target="tpu_custom_call" | custom-call | tf_op jit(solution)/shard_map/pallas_call | solution.py:418
Async XLA Ops:
  27.3 0.9 copy-start
  68.2 0.8 copy-start.1
  69.0 0.7 copy-start.2

commit v3 on v2

--- a/solution.py
+++ b/solution.py
@@ -81,6 +81,33 @@
             device_id=to_core[0],
             device_id_type=MESH,
         ).wait_recv()
+
+    if row_width:
+        holder = w // (wide // narrow)
+        first = pl.multiple_of(lax.rem(w, wide // narrow) * row_step, 128)
+        group = 2 * narrow
+
+    def row_copy(index, target, start, sem):
+        return pltpu.make_async_remote_copy(
+            src_ref=out.at[pl.ds(start, group), :, pl.ds(first, row_width)],
+            dst_ref=rows.at[pl.ds(start, group)],
+            send_sem=row_send.at[sem],
+            recv_sem=row_recv.at[index],
+            device_id=target,
+            device_id_type=MESH,
+        )
+
+    chips = [(zz, yy) for yy in [y] + ys for zz in [z] + zs]
+
+    def finish(number):
+        zz, yy = chips[number]
+        for nn in [n] + xs:
+            arrived(slot(zz, yy, 1 - core, nn))
+        if row_width:
+            @pl.when(n == holder)
+            def _():
+                for k, target in enumerate(to_x):
+                    row_copy(number, target, slot(zz, yy, 0, 0), number * len(to_x) + k).start()
 
     mine = slot(z, y, core, n)
     for target in to_x:
@@ -100,38 +127,18 @@
             arrived(index)
             for target in to_y + to_core:
                 send(out.at[index], index, target)
-    for yy in ys:
-        for zz in [z] + zs:
-            for nn in [n] + xs:
-                index = slot(zz, yy, core, nn)
-                arrived(index)
-                send(out.at[index], index, to_core[0])
     own.wait()
-
-    if row_width:
-        holder = w // (wide // narrow)
-        first = pl.multiple_of(lax.rem(w, wide // narrow) * row_step, 128)
-        group = 2 * narrow
-
-    def row_copy(index, target, start, sem):
-        return pltpu.make_async_remote_copy(
-            src_ref=out.at[pl.ds(start, group), :, pl.ds(first, row_width)],
-            dst_ref=rows.at[pl.ds(start, group)],
-            send_sem=row_send.at[sem],
-            recv_sem=row_recv.at[index],
-            device_id=target,
-            device_id_type=MESH,
-        )
-
-    chips = [(zz, yy) for yy in [y] + ys for zz in [z] + zs]
-    for number, (zz, yy) in enumerate(chips):
+    for number in range(outer):
+        finish(number)
+    for number, (zz, yy) in enumerate(chips[outer:], outer):
         for nn in [n] + xs:
-            arrived(slot(zz, yy, 1 - core, nn))
-        if row_width:
-            @pl.when(n == holder)
-            def _():
-                for k, target in enumerate(to_x):
-                    row_copy(number, target, slot(zz, yy, 0, 0), number * len(to_x) + k).start()
+            index = slot(zz, yy, core, nn)
+            arrived(index)
+            send(out.at[index], index, to_core[0])
+        if number > outer:
+            finish(number - 1)
+    if len(chips) > outer:
+        finish(len(chips) - 1)
 
     for copy in started:
         copy.wait_send()

time: 94.4 us -> 86.8 us (0.919)
  Pallas kernels: 90.9 us -> 83.2 us
    pallas_call x2, Pallas kernels: 55.7 us -> 47.9 us  [gather(): pl.pallas_call(functools.partial(gather_kernel, wide, narrow, split, row_...]
where the time goes in v3:
time: 86.8 us; the launch traced here: 86.4 us
  Pallas kernels  83.2 us (96%)
  local copies, waits for them, and re-layouts  2.38 us (3%)
    pallas_call x2, Pallas kernels, gather(): pl.pallas_call(functools.partial(gather_kernel, wide, narrow, split, row_...  47.9 us
    pallas_call x1, Pallas kernels, chi_of(): pl.pallas_call(functools.partial(chi_kernel, eps_cond.shape[0], eps_val.s...  24.4 us
    pallas_call x1, Pallas kernels, transform_pairs(): pl.pallas_call(functools.partial(pair_kernel, reach, 256), out_shape=jax....  10.9 us
    unnamed x6, local copies, waits for them, and re-layouts  2.38 us

profile of v3, /device:TPU:14, one launch (start us, length us, event | category | flops | bytes accessed | tf_op | source)
XLA Modules:
  0.0 86.4 jit_solution(12968637847588192184)
XLA Ops:
  0.0 0.8 pad_maximum_fusion.scalars
  0.8 15.8 %shard_map.127.refs_0_ = f32[32,8,1024]{2,1,0:T(8,128)} custom-call(f32[8,1024]{1,0:T(8,128)} %src.1), custom_call_target="tpu_custom_call" | custom-call | tf_op jit(solution)/shard_map/pallas_call | solution.py:176
  16.6 10.9 %shard_map.128.src = bf16[16,4608]{1,0:T(8,128)(2,1)} custom-call(f32[32,8,1024]{2,1,0:T(8,128)} %shard_map.127.refs_0_, f32[32,1,1024]{2,1,0:T(1,128)} %bitcast.7, bf16[1024,512]{1,0:T(8,128)(2,1)} %constant.14.clone.refs_2_, bf16[1024,512]{1,0:T(8,128)(2,1)} %constant.15.clone.refs_3_, bf16[2,200,256]{2,1,0:T(8,128)(2,1)} %constant.16.clone.refs_4_, ...), custom_call_target="tpu_custom_call" | custom-call | tf_op jit(solution)/shard_map/pallas_call | solution.py:341
  27.5 0.0 copy-start
  27.5 0.9 %copy-done = bf16[16,4608]{1,0:T(8,128)(2,1)S(1)} copy-done((bf16[16,4608]{1,0:T(8,128)(2,1)S(1)}, bf16[16,4608]{1,0:T(8,128)(2,1)}, u32[]{:S(2)}) %copy-start) | copy-done | bytes 147480
  28.4 32.1 %shard_map.129 = (bf16[32,16,2304]{2,1,0:T(8,128)(2,1)S(1)}, bf16[32,16,512]{2,1,0:T(8,128)(2,1)S(1)}) custom-call(bf16[16,4608]{1,0:T(8,128)(2,1)S(1)} %copy-done), custom_call_target="tpu_custom_call" | custom-call | tf_op jit(solution)/shard_map/pallas_call | solution.py:176
  60.5 0.0 copy-start.1
  60.5 0.7 copy-done.1
  61.3 0.0 copy-start.2
  61.3 0.7 copy-done.2
  62.0 24.4 %shard_map.130 = f32[6,512,4096]{2,1,0:T(8,128)} custom-call(f32[46]{0:T(128)S(1)} %pad_maximum_fusion.scalars, s32[1,8192]{1,0:T(1,128)S(1)} %bitcast.6, s32[2,1,2304]{2,1,0:T(1,128)S(1)} %copy-done.2, bf16[512,512]{1,0:T(8,128)(2,1)S(1)} %bitcast.5, bf16[512,2304]{1,0:T(8,128)(2,1)S(1)} %bitcast.4), custom_call_target="tpu_custom_call" | custom-call | tf_op jit(solution)/shard_map/pallas_call | solution.py:425
Async XLA Ops:
  27.5 0.9 %copy-start = (bf16[16,4608]{1,0:T(8,128)(2,1)S(1)}, bf16[16,4608]{1,0:T(8,128)(2,1)}, u32[]{:S(2)}) copy-start(bf16[16,4608]{1,0:T(8,128)(2,1)} %shard_map.128.src) | copy-start | bytes 442372
  60.5 0.8 copy-start.1
  61.3 0.7 copy-start.2

commit v4 on v3

--- a/solution.py
+++ b/solution.py
@@ -289,15 +289,19 @@
     for copy in copies:
         copy.start()
     val, cond, plane_h, plane_l, line_h, line_l, codes, gmap = held
-    for copy in copies:
-        copy.wait()
     xs, num_val, plane = val.shape
     count = codes.shape[0]
     kinds = 2 * reach + 1
+    copies[0].wait()
+    copies[1].wait()
     field[...] = (val[...] * cond[...]).reshape(xs * num_val, plane)
+    copies[2].wait()
+    copies[3].wait()
     step = dot3(field[...], plane_h[...], plane_l[...])
     real, imag = step[:, :count], step[:, count:]
     size = kinds * num_val
+    for copy in copies[4:]:
+        copy.wait()
     cos_h, sin_h, cos_l, sin_l = line_h[0], line_h[1], line_l[0], line_l[1]
     picked[:size, :] = dot3_left(cos_h, cos_l, real) + dot3_left(sin_h, sin_l, imag)
     picked[size:, :] = dot3_left(cos_h, cos_l, imag) - dot3_left(sin_h, sin_l, real)
@@ -339,7 +343,7 @@
     operands = (val, cond, plane_h, plane_l, line_h, line_l, codes, gmap)
     held = [pltpu.VMEM(x.shape, x.dtype) for x in operands]
     return pl.pallas_call(
-        functools.partial(pair_kernel, reach, 256),
+        functools.partial(pair_kernel, reach, 512 if waves % 512 == 0 else 256),
         out_shape=jax.ShapeDtypeStruct((2 * num_val, waves), jnp.bfloat16),
         in_specs=[pl.BlockSpec(memory_space=pl.ANY)] * 8,
         out_specs=pl.BlockSpec(memory_space=VMEM),

time: 86.8 us -> 84.2 us (0.970)
  Pallas kernels: 83.2 us -> 80.6 us
    pallas_call x1, Pallas kernels: 10.9 us -> 8 us  [transform_pairs(): pl.pallas_call(functools.partial(pair_kernel, reach, 512 if waves % 512 =...]
where the time goes in v4:
time: 84.2 us; the launch traced here: 83.8 us
  Pallas kernels  80.6 us (96%)
  local copies, waits for them, and re-layouts  2.38 us (3%)
    pallas_call x2, Pallas kernels, gather(): pl.pallas_call(functools.partial(gather_kernel, wide, narrow, split, row_...  48.2 us
    pallas_call x1, Pallas kernels, chi_of(): pl.pallas_call(functools.partial(chi_kernel, eps_cond.shape[0], eps_val.s...  24.4 us
    pallas_call x1, Pallas kernels, transform_pairs(): pl.pallas_call(functools.partial(pair_kernel, reach, 512 if waves % 512 =...  8 us
    unnamed x6, local copies, waits for them, and re-layouts  2.38 us

profile of v4, /device:TPU:14, one launch (start us, length us, event | category | flops | bytes accessed | tf_op | source)
XLA Modules:
  0.0 83.8 jit_solution(16302438596669603269)
XLA Ops:
  0.0 0.8 pad_maximum_fusion.scalars
  0.8 15.8 %shard_map.127.refs_0_ = f32[32,8,1024]{2,1,0:T(8,128)} custom-call(f32[8,1024]{1,0:T(8,128)} %src.1), custom_call_target="tpu_custom_call" | custom-call | tf_op jit(solution)/shard_map/pallas_call | solution.py:176
  16.6 8.0 %shard_map.128.src = bf16[16,4608]{1,0:T(8,128)(2,1)} custom-call(f32[32,8,1024]{2,1,0:T(8,128)} %shard_map.127.refs_0_, f32[32,1,1024]{2,1,0:T(1,128)} %bitcast.7, bf16[1024,512]{1,0:T(8,128)(2,1)} %constant.14.clone.refs_2_, bf16[1024,512]{1,0:T(8,128)(2,1)} %constant.15.clone.refs_3_, bf16[2,200,256]{2,1,0:T(8,128)(2,1)} %constant.16.clone.refs_4_, ...), custom_call_target="tpu_custom_call" | custom-call | tf_op jit(solution)/shard_map/pallas_call | solution.py:345
  24.6 0.0 copy-start
  24.6 0.9 %copy-done = bf16[16,4608]{1,0:T(8,128)(2,1)S(1)} copy-done((bf16[16,4608]{1,0:T(8,128)(2,1)S(1)}, bf16[16,4608]{1,0:T(8,128)(2,1)}, u32[]{:S(2)}) %copy-start) | copy-done | bytes 147480
  25.5 32.4 %shard_map.129 = (bf16[32,16,2304]{2,1,0:T(8,128)(2,1)S(1)}, bf16[32,16,512]{2,1,0:T(8,128)(2,1)S(1)}) custom-call(bf16[16,4608]{1,0:T(8,128)(2,1)S(1)} %copy-done), custom_call_target="tpu_custom_call" | custom-call | tf_op jit(solution)/shard_map/pallas_call | solution.py:176
  57.9 0.0 copy-start.1
  57.9 0.7 copy-done.1
  58.6 0.0 copy-start.2
  58.6 0.7 copy-done.2
  59.4 24.4 %shard_map.130 = f32[6,512,4096]{2,1,0:T(8,128)} custom-call(f32[46]{0:T(128)S(1)} %pad_maximum_fusion.scalars, s32[1,8192]{1,0:T(1,128)S(1)} %bitcast.6, s32[2,1,2304]{2,1,0:T(1,128)S(1)} %copy-done.2, bf16[512,512]{1,0:T(8,128)(2,1)S(1)} %bitcast.5, bf16[512,2304]{1,0:T(8,128)(2,1)S(1)} %bitcast.4), custom_call_target="tpu_custom_call" | custom-call | tf_op jit(solution)/shard_map/pallas_call | solution.py:429
Async XLA Ops:
  24.6 0.9 %copy-start = (bf16[16,4608]{1,0:T(8,128)(2,1)S(1)}, bf16[16,4608]{1,0:T(8,128)(2,1)}, u32[]{:S(2)}) copy-start(bf16[16,4608]{1,0:T(8,128)(2,1)} %shard_map.128.src) | copy-start | bytes 442372
  57.9 0.8 copy-start.1
  58.6 0.7 copy-start.2
